TPU v7x, 32 devices: a whole 2x2x4 slice. The times are simulated.
32 devices in a mesh: slab: 2 (over x), blk: 16 (over z, y, core).
Axes of the slice: x: 2, y: 2, z: 4, core: 2. Of those that a mesh axis runs over, the one named last changes fastest.
Arguments:
- transmit: bfloat16 [2, 1024, 2048], P('slab', 'blk'), may hold values from -0.125 to 0.125
- reflect: bfloat16 [2, 2, 1024, 2048], P('slab', None, 'blk'), may hold values from -0.07910156 to 0.07910156
- source_amp: bfloat16 [512, 2048], P('blk'), may hold values from -6 to 6
- source_cell: int32 [512], P('blk'), may hold values from 0 to 1023
- source_slab: int32 [512], P('blk'), may hold values from 0 to 1
Outputs:
- sweep_out: float32 [2, 512, 2048], P('slab', 'blk')
All inputs are finite; a program needn't handle non-finite values.
Results may differ from a plain program's by a relative error of at most 0.018.
Values may be sent and summed in bfloat16 or wider, within the bound.
A program may use at most 64 MiB of HBM per device.

v0:
```python
import jax
import jax.numpy as jnp
from jax import lax
from jax.sharding import PartitionSpec as P


def shifted(block, axis, distance):
    devices = range(lax.axis_size(axis))
    route = [(i - distance, i) for i in devices if i - distance in devices]
    return lax.ppermute(block, axis, route)


def transposed(matrix):
    half_width = matrix.shape[0]
    return jnp.concatenate([matrix[:, :half_width].T, matrix[:, half_width:].T], 1)


def complex_rows(left_rows, right_matrix):
    inner_width = right_matrix.shape[0]
    outer_width = right_matrix.shape[1] // 2
    row_count = left_rows.shape[0]
    stacked = jnp.concatenate([left_rows[:, :inner_width], left_rows[:, inner_width:]], 0)
    product = jnp.dot(stacked, right_matrix, preferred_element_type=jnp.float32)
    real_out = product[:row_count, :outer_width] - product[row_count:, outer_width:]
    imag_out = product[:row_count, outer_width:] + product[row_count:, :outer_width]
    return jnp.concatenate([real_out, imag_out], 1)


def body(transmit, reflect, source_amp, source_cell, source_slab):
    trans_local = transmit[0]
    refl_local = reflect[0]
    half_width = source_amp.shape[1] // 2
    refl_second = lax.all_gather(refl_local[1], "blk", axis=0, tiled=True)
    coupling = complex_rows(refl_local[0], refl_second).astype(jnp.bfloat16)
    start_rows = trans_local.astype(jnp.float32)
    piece_rows = lax.all_gather(trans_local, "blk", axis=0, tiled=True)
    piece_count = piece_rows.shape[0]
    real_cols = lax.slice_in_dim(coupling, 0, piece_count, axis=1)
    imag_cols = lax.dynamic_slice_in_dim(coupling, half_width, piece_count, 1)
    left_rows = jnp.concatenate([real_cols, imag_cols], 1)
    joined = (start_rows + complex_rows(left_rows, piece_rows)).astype(jnp.bfloat16)
    slab_matrix = lax.all_gather(joined, "blk", axis=0, tiled=True)
    back_matrix = transposed(slab_matrix)
    cell_index = lax.iota(jnp.int32, half_width)
    offset = (cell_index[None, :] - source_cell[:, None]) % half_width
    inside = offset < half_width // 4
    here = source_slab == lax.axis_index("slab")
    keep = inside & here[:, None]
    keep = jnp.concatenate([keep, keep], 1)
    forcing = jnp.where(keep, source_amp, jnp.zeros_like(source_amp))
    chain_length = lax.axis_size("slab")
    carried = forcing
    for sweep_step in range(chain_length - 1):
        arrived = shifted(carried, "slab", 1)
        carried = (forcing.astype(jnp.float32) + complex_rows(arrived, slab_matrix)).astype(
            jnp.bfloat16
        )
    current = carried.astype(jnp.float32)
    for sweep_step in range(chain_length - 1):
        message = complex_rows(current.astype(jnp.bfloat16), back_matrix).astype(jnp.bfloat16)
        arrived = shifted(message, "slab", -1)
        current = carried.astype(jnp.float32) + arrived.astype(jnp.float32)
    return current[None]


def solution(mesh):
    return jax.shard_map(
        body,
        mesh=mesh,
        in_specs=(
            P("slab", "blk", None),
            P("slab", None, "blk", None),
            P("blk", None),
            P("blk"),
            P("blk"),
        ),
        out_specs=P("slab", "blk", None),
        check_vma=False,
    )
```

profile of v0, /device:TPU:0, one launch (start us, length us, event | category | flops | bytes accessed | tf_op | source)
XLA Modules:
  0.0 186.9 jit_solution(4141823036874665269)
XLA Ops:
  6.5 0.0 all-gather.8.cloned.1.call-start
  6.5 1.8 slice_bitcast_fusion.2
  8.3 0.0 all-gather.8.cloned.1.call-update
  8.3 0.0 all-gather.10.cloned.1.call-start
  8.4 0.7 all-gather.10.cloned.1.call-update
  9.1 0.0 all-gather.6.cloned.1.call-start
  9.2 53.5 %all-gather.8.cloned.1.call-done = bf16[1,1,1024,2048]{3,2,1,0:T(8,128)(2,1)} async-done(((bf16[1,1,64,2048]{3,2,1,0:T(8,128)(2,1)}), bf16[1,1,1024,2048]{3,2,1,0:T(8,128)(2,1)}) %all-gather.8.cloned.1.call-update) | async-done | bytes 4194320 | tf_op jit(solution)/shard_map/all_gather | solution.py:33
  62.6 2.9 %fusion.6 = f32[128,2048]{1,0:T(8,128)S(1)} fusion(bf16[1,1,1024,2048]{3,2,1,0:T(8,128)(2,1)} %all-gather.8.cloned.1.call-done, bf16[64,1024]{1,0:T(8,128)(2,1)S(1)} %get-tuple-element.18, bf16[64,1024]{1,0:T(8,128)(2,1)S(1)} %get-tuple-element.17), kind=kOutput, calls=%fused_computation.6 | convolution fusion | flops 537395200 | bytes 5505024 | tf_op jit(solution)/shard_map/dot_general | solution.py:23
  65.5 0.0 copy-start.1
  65.5 0.1 fusion.10
  65.6 48.1 %all-gather.10.cloned.1.call-done = bf16[1,1024,2048]{2,1,0:T(8,128)(2,1)} async-done(((bf16[1,64,2048]{2,1,0:T(8,128)(2,1)}), bf16[1,1024,2048]{2,1,0:T(8,128)(2,1)}) %all-gather.10.cloned.1.call-update) | async-done | bytes 4194320 | tf_op jit(solution)/shard_map/all_gather | solution.py:36
  113.7 0.0 copy-start.4
  113.7 0.0 copy-start.3
  113.7 0.0 copy-start.2
  113.7 2.9 %fusion.4 = f32[128,2048]{1,0:T(8,128)S(1)} fusion(bf16[1,1024,2048]{2,1,0:T(8,128)(2,1)} %all-gather.10.cloned.1.call-done, bf16[64,1024]{1,0:T(8,128)(2,1)S(1)} %get-tuple-element.10, bf16[64,1024]{1,0:T(8,128)(2,1)S(1)} %get-tuple-element.9), kind=kOutput, calls=%fused_computation.4 | convolution fusion | flops 537395200 | bytes 5505024 | tf_op jit(solution)/shard_map/dot_general | solution.py:23
  116.7 0.1 slice_subtract_fusion
  116.7 0.0 copy-done.1
  116.8 0.8 fusion.8
  117.5 0.0 all-gather.6.cloned.1.call-update
  117.6 0.0 copy-done.4
  117.6 0.0 copy-done.3
  117.6 0.1 fusion.32
  117.7 0.0 copy-done.2
  117.8 3.4 %collective-permute-start = (bf16[32,2048]{1,0:T(8,128)(2,1)S(1)}, bf16[32,2048]{1,0:T(8,128)(2,1)S(1)}, u32[]{:S(2)}, u32[]{:S(2)}) collective-permute-start(bf16[32,2048]{1,0:T(8,128)(2,1)S(1)} %add_select_fusion), channel_id=1, source_target_pairs={{0,16},{1,17},{2,18},{3,19},{4,20},{5,21},{6,22},{7,23},{8,24},{9,... | collective-permute-start | bytes 393224 | tf_op jit(solution)/shard_map/ppermute | solution.py:10
  121.2 3.1 %collective-permute-done = bf16[32,2048]{1,0:T(8,128)(2,1)S(1)} collective-permute-done((bf16[32,2048]{1,0:T(8,128)(2,1)S(1)}, bf16[32,2048]{1,0:T(8,128)(2,1)S(1)}, u32[]{:S(2)}, u32[]{:S(2)}) %collective-permute-start) | collective-permute-done | bytes 131104 | tf_op jit(solution)/shard_map/ppermute | solution.py:10
  124.3 42.3 %all-gather.6.cloned.1.call-done = bf16[1024,2048]{1,0:T(8,128)(2,1)} async-done(((bf16[64,2048]{1,0:T(8,128)(2,1)}), bf16[1024,2048]{1,0:T(8,128)(2,1)}) %all-gather.6.cloned.1.call-update) | async-done | bytes 4194320 | tf_op jit(solution)/shard_map/all_gather | solution.py:42
  166.6 0.0 copy-start
  166.6 3.2 %fusion.22 = f32[64,2048]{1,0:T(8,128)S(1)} fusion(bf16[1024,2048]{1,0:T(8,128)(2,1)} %all-gather.6.cloned.1.call-done, bf16[32,1024]{1,0:T(8,128)(2,1)S(1)} %get-tuple-element.22, bf16[32,1024]{1,0:T(8,128)(2,1)S(1)} %get-tuple-element.21), kind=kOutput, calls=%fused_computation.40 | convolution fusion | flops 268697600 | bytes 4849664 | tf_op jit(solution)/shard_map/dot_general | solution.py:23
  169.9 0.2 copy-done
  170.1 0.5 slice_bitcast_fusion.1
  170.6 1.4 fusion
  172.1 1.3 collective-permute-start.1
  173.4 6.2 %collective-permute-done.1 = bf16[32,2048]{1,0:T(8,128)(2,1)S(1)} collective-permute-done((bf16[32,2048]{1,0:T(8,128)(2,1)S(1)}, bf16[32,2048]{1,0:T(8,128)(2,1)S(1)}, u32[]{:S(2)}, u32[]{:S(2)}) %collective-permute-start.1) | collective-permute-done | bytes 131104 | tf_op jit(solution)/shard_map/ppermute | solution.py:10
  179.6 0.7 add_bitcast_fusion
  (9 shorter events, 0.2 us)
Async XLA Ops:
  6.5 56.1 %all-gather.8.cloned.1.call-start = ((), (), s32[]{:S(2)}) async-start(), calls=%async_computation.1 | async-start | bytes 4456448 | tf_op jit(solution)/shard_map/all_gather | solution.py:33
  8.3 105.4 %all-gather.10.cloned.1.call-start = ((), (), s32[]{:S(2)}) async-start(), calls=%async_computation.2 | async-start | bytes 4456448 | tf_op jit(solution)/shard_map/all_gather | solution.py:36
  9.1 157.5 %all-gather.6.cloned.1.call-start = ((), (), s32[]{:S(2)}) async-start(), calls=%async_computation | async-start | bytes 4456448 | tf_op jit(solution)/shard_map/all_gather | solution.py:42
  65.5 51.2 %copy-start.1 = (bf16[1,64,2048]{2,1,0:T(8,128)(2,1)S(1)}, bf16[1,64,2048]{2,1,0:T(8,128)(2,1)}, u32[]{:S(2)}) copy-start(bf16[1,64,2048]{2,1,0:T(8,128)(2,1)} %param.5) | copy-start | bytes 786436
  113.7 3.8 %copy-start.4 = (s32[32]{0:T(128)S(1)}, s32[32]{0:T(128)}, u32[]{:S(2)}) copy-start(s32[32]{0:T(128)} %param.9) | copy-start | bytes 388
  113.7 3.9 %copy-start.3 = (s32[32]{0:T(128)S(1)}, s32[32]{0:T(128)}, u32[]{:S(2)}) copy-start(s32[32]{0:T(128)} %param.8) | copy-start | bytes 388
  113.7 4.0 %copy-start.2 = (bf16[32,2048]{1,0:T(8,128)(2,1)S(1)}, bf16[32,2048]{1,0:T(8,128)(2,1)}, u32[]{:S(2)}) copy-start(bf16[32,2048]{1,0:T(8,128)(2,1)} %param.7) | copy-start | bytes 393220
  117.8 6.5 %collective-permute-start = (bf16[32,2048]{1,0:T(8,128)(2,1)S(1)}, bf16[32,2048]{1,0:T(8,128)(2,1)S(1)}, u32[]{:S(2)}, u32[]{:S(2)}) collective-permute-start(bf16[32,2048]{1,0:T(8,128)(2,1)S(1)} %add_select_fusion), channel_id=1, source_target_pairs={{0,16},{1,17},{2,18},{3,19},{4,20},{5,21},{6,22},{7,23},{8,24},{9,... | collective-permute-start | bytes 393224 | tf_op jit(solution)/shard_map/ppermute | solution.py:10
  166.6 3.4 %copy-start = (bf16[1024,2048]{1,0:T(8,128)(2,1)S(1)}, bf16[1024,2048]{1,0:T(8,128)(2,1)}, u32[]{:S(2)}) copy-start(bf16[1024,2048]{1,0:T(8,128)(2,1)} %all-gather.6.cloned.1.call-done) | copy-start | bytes 12582916
  172.1 7.5 %collective-permute-start.1 = (bf16[32,2048]{1,0:T(8,128)(2,1)S(1)}, bf16[32,2048]{1,0:T(8,128)(2,1)S(1)}, u32[]{:S(2)}, u32[]{:S(2)}) collective-permute-start(bf16[32,2048]{1,0:T(8,128)(2,1)S(1)} %pad_maximum_fusion), channel_id=1, source_target_pairs={{16,0},{17,1},{18,2},{19,3},{20,4},{21,5},{22,6},{23,7},{24,8},{25... | collective-permute-start | bytes 393224 | tf_op jit(solution)/shard_map/ppermute | solution.py:10
Sparse Core Ops, SparseCore 0:
  9.5 53.0 all-gather.7
  64.8 48.8 all-gather.9
  117.7 48.8 all-gather.5
where the time goes:
time: 187 us
  waiting for transfers between devices  154 us (82%)
  between operations  13.3 us (7%)
  matrix products  10.4 us (6%)
  starting transfers between devices  4.75 us (3%)
  local copies, waits for them, and re-layouts  2.53 us (1%)
  other arithmetic  1.89 us (1%)
    all_gather x1, waiting for transfers between devices, body(): refl_second = lax.all_gather(refl_local[1], 'blk', axis=0, tiled=True)  53.5 us
    all_gather x1, waiting for transfers between devices, body(): piece_rows = lax.all_gather(trans_local, 'blk', axis=0, tiled=True)  48.1 us
    all_gather x1, waiting for transfers between devices, body(): slab_matrix = lax.all_gather(joined, 'blk', axis=0, tiled=True)  42.3 us
    dot_general x4, matrix products, complex_rows(): product = jnp.dot(stacked, right_matrix, preferred_element_type=jnp.float32)  10.4 us
    ppermute x2, waiting for transfers between devices, shifted(): return lax.ppermute(block, axis, route)  9.38 us
    ppermute x2, starting transfers between devices, shifted(): return lax.ppermute(block, axis, route)  4.67 us
  transfers between devices with their start and end apart: 5, of which 5 were waited for; matrix products, arithmetic and copies ran while one was open for 2% of the time, Pallas kernels for 0%

commit v1 on v0

--- a/solution.py
+++ b/solution.py
@@ -33,7 +33,12 @@
     refl_second = lax.all_gather(refl_local[1], "blk", axis=0, tiled=True)
     coupling = complex_rows(refl_local[0], refl_second).astype(jnp.bfloat16)
     start_rows = trans_local.astype(jnp.float32)
-    piece_rows = lax.all_gather(trans_local, "blk", axis=0, tiled=True)
+    ring = [trans_local]
+    for hop in range(15):
+        ring.append(lax.ppermute(ring[-1], "blk", [(dev, (dev + 1) % 16) for dev in range(16)]))
+    piece_rows = jnp.roll(
+        jnp.concatenate(ring[::-1], axis=0), (lax.axis_index("blk") + 1) * ring[0].shape[0], axis=0
+    )
     piece_count = piece_rows.shape[0]
     real_cols = lax.slice_in_dim(coupling, 0, piece_count, axis=1)
     imag_cols = lax.dynamic_slice_in_dim(coupling, half_width, piece_count, 1)

time: 187 us -> 258 us (1.38)
  waiting for transfers between devices: 154 us -> 194 us
  local copies, waits for them, and re-layouts: 2.53 us -> 32.9 us
    ppermute x0 -> x15, waiting for transfers between devices: none -> 125 us  [body(): lax.ppermute(ring[-1], 'blk', [(dev, (dev + 1) % 16) for dev in range(16)])]
    all_gather x1 -> x0, waiting for transfers between devices: 48.1 us -> none  [body(): piece_rows = lax.all_gather(trans_local, 'blk', axis=0, tiled=True)]
    all_gather x1, waiting for transfers between devices: 53.5 us -> 17.2 us  [body(): refl_second = lax.all_gather(refl_local[1], 'blk', axis=0, tiled=True)]
    unnamed x10 -> x45, local copies, waits for them, and re-layouts: 0.19 us -> 28.1 us
  transfers between devices with their start and end apart: 5 -> 19, of which waited for: 5 -> 19; matrix products, arithmetic and copies ran while one was open for 2% -> 12% of each run, Pallas kernels for 0% -> 0%
where the time goes in v1:
time: 258 us
  waiting for transfers between devices  194 us (75%)
  local copies, waits for them, and re-layouts  32.9 us (13%)
  between operations  13.6 us (5%)
  matrix products  10.5 us (4%)
  starting transfers between devices  5.24 us (2%)
    ppermute x15, waiting for transfers between devices, body(): lax.ppermute(ring[-1], 'blk', [(dev, (dev + 1) % 16) for dev in range(16)])  125 us
    all_gather x1, waiting for transfers between devices, body(): slab_matrix = lax.all_gather(joined, 'blk', axis=0, tiled=True)  42.3 us
    unnamed x45, local copies, waits for them, and re-layouts  28.1 us
    all_gather x1, waiting for transfers between devices, body(): refl_second = lax.all_gather(refl_local[1], 'blk', axis=0, tiled=True)  17.2 us
    dot_general x4, matrix products, complex_rows(): product = jnp.dot(stacked, right_matrix, preferred_element_type=jnp.float32)  10.5 us
    ppermute x2, waiting for transfers between devices, shifted(): return lax.ppermute(block, axis, route)  9.37 us
  transfers between devices with their start and end apart: 19, of which 19 were waited for; matrix products, arithmetic and copies ran while one was open for 12% of the time, Pallas kernels for 0%

profile of v1, /device:TPU:0, one launch (start us, length us, event | category | flops | bytes accessed | tf_op | source)
XLA Modules:
  0.0 258.0 jit_solution(14535312208968174957)
XLA Ops:
  6.5 0.5 collective-permute-start.1
  7.0 9.3 %collective-permute-done.1 = bf16[64,2048]{1,0:T(8,128)(2,1)S(1)} collective-permute-done((bf16[64,2048]{1,0:T(8,128)(2,1)}, bf16[64,2048]{1,0:T(8,128)(2,1)S(1)}, u32[]{:S(2)}, u32[]{:S(2)}) %collective-permute-start.1) | collective-permute-done | bytes 262176 | tf_op jit(solution)/shard_map/ppermute | solution.py:38
  16.3 8.5 %collective-permute-done.2 = bf16[64,2048]{1,0:T(8,128)(2,1)S(1)} collective-permute-done((bf16[64,2048]{1,0:T(8,128)(2,1)S(1)}, bf16[64,2048]{1,0:T(8,128)(2,1)S(1)}, u32[]{:S(2)}, u32[]{:S(2)}) %collective-permute-start.2) | collective-permute-done | bytes 262176 | tf_op jit(solution)/shard_map/ppermute | solution.py:38
  24.8 8.5 %collective-permute-done.3 = bf16[64,2048]{1,0:T(8,128)(2,1)S(1)} collective-permute-done((bf16[64,2048]{1,0:T(8,128)(2,1)S(1)}, bf16[64,2048]{1,0:T(8,128)(2,1)S(1)}, u32[]{:S(2)}, u32[]{:S(2)}) %collective-permute-start.3) | collective-permute-done | bytes 262176 | tf_op jit(solution)/shard_map/ppermute | solution.py:38
  33.3 8.5 %collective-permute-done.4 = bf16[64,2048]{1,0:T(8,128)(2,1)S(1)} collective-permute-done((bf16[64,2048]{1,0:T(8,128)(2,1)S(1)}, bf16[64,2048]{1,0:T(8,128)(2,1)S(1)}, u32[]{:S(2)}, u32[]{:S(2)}) %collective-permute-start.4) | collective-permute-done | bytes 262176 | tf_op jit(solution)/shard_map/ppermute | solution.py:38
  41.8 8.5 %collective-permute-done.5 = bf16[64,2048]{1,0:T(8,128)(2,1)S(1)} collective-permute-done((bf16[64,2048]{1,0:T(8,128)(2,1)S(1)}, bf16[64,2048]{1,0:T(8,128)(2,1)S(1)}, u32[]{:S(2)}, u32[]{:S(2)}) %collective-permute-start.5) | collective-permute-done | bytes 262176 | tf_op jit(solution)/shard_map/ppermute | solution.py:38
  50.3 8.5 %collective-permute-done.6 = bf16[64,2048]{1,0:T(8,128)(2,1)S(1)} collective-permute-done((bf16[64,2048]{1,0:T(8,128)(2,1)S(1)}, bf16[64,2048]{1,0:T(8,128)(2,1)S(1)}, u32[]{:S(2)}, u32[]{:S(2)}) %collective-permute-start.6) | collective-permute-done | bytes 262176 | tf_op jit(solution)/shard_map/ppermute | solution.py:38
  58.8 8.5 %collective-permute-done.7 = bf16[64,2048]{1,0:T(8,128)(2,1)S(1)} collective-permute-done((bf16[64,2048]{1,0:T(8,128)(2,1)S(1)}, bf16[64,2048]{1,0:T(8,128)(2,1)S(1)}, u32[]{:S(2)}, u32[]{:S(2)}) %collective-permute-start.7) | collective-permute-done | bytes 262176 | tf_op jit(solution)/shard_map/ppermute | solution.py:38
  67.3 8.5 %collective-permute-done.8 = bf16[64,2048]{1,0:T(8,128)(2,1)S(1)} collective-permute-done((bf16[64,2048]{1,0:T(8,128)(2,1)S(1)}, bf16[64,2048]{1,0:T(8,128)(2,1)S(1)}, u32[]{:S(2)}, u32[]{:S(2)}) %collective-permute-start.8) | collective-permute-done | bytes 262176 | tf_op jit(solution)/shard_map/ppermute | solution.py:38
  75.8 8.5 %collective-permute-done.9 = bf16[64,2048]{1,0:T(8,128)(2,1)S(1)} collective-permute-done((bf16[64,2048]{1,0:T(8,128)(2,1)S(1)}, bf16[64,2048]{1,0:T(8,128)(2,1)S(1)}, u32[]{:S(2)}, u32[]{:S(2)}) %collective-permute-start.9) | collective-permute-done | bytes 262176 | tf_op jit(solution)/shard_map/ppermute | solution.py:38
  84.3 8.5 %collective-permute-done.10 = bf16[64,2048]{1,0:T(8,128)(2,1)S(1)} collective-permute-done((bf16[64,2048]{1,0:T(8,128)(2,1)S(1)}, bf16[64,2048]{1,0:T(8,128)(2,1)S(1)}, u32[]{:S(2)}, u32[]{:S(2)}) %collective-permute-start.10) | collective-permute-done | bytes 262176 | tf_op jit(solution)/shard_map/ppermute | solution.py:38
  92.8 8.5 %collective-permute-done.11 = bf16[64,2048]{1,0:T(8,128)(2,1)S(1)} collective-permute-done((bf16[64,2048]{1,0:T(8,128)(2,1)S(1)}, bf16[64,2048]{1,0:T(8,128)(2,1)S(1)}, u32[]{:S(2)}, u32[]{:S(2)}) %collective-permute-start.11) | collective-permute-done | bytes 262176 | tf_op jit(solution)/shard_map/ppermute | solution.py:38
  101.3 8.5 %collective-permute-done.12 = bf16[64,2048]{1,0:T(8,128)(2,1)S(1)} collective-permute-done((bf16[64,2048]{1,0:T(8,128)(2,1)S(1)}, bf16[64,2048]{1,0:T(8,128)(2,1)S(1)}, u32[]{:S(2)}, u32[]{:S(2)}) %collective-permute-start.12) | collective-permute-done | bytes 262176 | tf_op jit(solution)/shard_map/ppermute | solution.py:38
  109.8 8.5 %collective-permute-done.13 = bf16[64,2048]{1,0:T(8,128)(2,1)S(1)} collective-permute-done((bf16[64,2048]{1,0:T(8,128)(2,1)S(1)}, bf16[64,2048]{1,0:T(8,128)(2,1)S(1)}, u32[]{:S(2)}, u32[]{:S(2)}) %collective-permute-start.13) | collective-permute-done | bytes 262176 | tf_op jit(solution)/shard_map/ppermute | solution.py:38
  118.3 0.7 copy-done.2
  119.0 8.6 %collective-permute-done.14 = bf16[64,2048]{1,0:T(8,128)(2,1)} collective-permute-done((bf16[64,2048]{1,0:T(8,128)(2,1)S(1)}, bf16[64,2048]{1,0:T(8,128)(2,1)}, u32[]{:S(2)}, u32[]{:S(2)}) %collective-permute-start.14) | collective-permute-done | bytes 262176 | tf_op jit(solution)/shard_map/ppermute | solution.py:38
  127.6 1.9 slice_bitcast_fusion.2
  129.6 1.6 fusion.38
  131.2 5.2 %collective-permute-done.15 = bf16[64,2048]{1,0:T(8,128)(2,1)} collective-permute-done((bf16[64,2048]{1,0:T(8,128)(2,1)}, bf16[64,2048]{1,0:T(8,128)(2,1)}, u32[]{:S(2)}, u32[]{:S(2)}) %collective-permute-start.15) | collective-permute-done | bytes 262176 | tf_op jit(solution)/shard_map/ppermute | solution.py:38
  136.4 1.7 constant_dynamic-update-slice_fusion.31
  138.1 1.7 constant_dynamic-update-slice_fusion.30
  139.7 1.7 constant_dynamic-update-slice_fusion.29
  141.4 0.7 constant_dynamic-update-slice_fusion.28
  142.1 0.7 constant_dynamic-update-slice_fusion.27
  142.8 0.7 constant_dynamic-update-slice_fusion.26
  143.6 0.7 constant_dynamic-update-slice_fusion.25
  144.3 0.7 constant_dynamic-update-slice_fusion.24
  145.0 0.7 constant_dynamic-update-slice_fusion.23
  145.7 0.7 constant_dynamic-update-slice_fusion.22
  146.5 0.7 constant_dynamic-update-slice_fusion.21
  147.2 0.7 constant_dynamic-update-slice_fusion.20
  147.9 0.7 constant_dynamic-update-slice_fusion.19
  148.6 0.7 constant_dynamic-update-slice_fusion.18
  149.3 0.7 constant_dynamic-update-slice_fusion.17
  150.0 0.7 constant_dynamic-update-slice_fusion.16
  150.8 1.7 constant_dynamic-update-slice_fusion.15
  152.5 1.7 constant_dynamic-update-slice_fusion.14
  154.2 0.7 constant_dynamic-update-slice_fusion.13
  154.9 0.7 constant_dynamic-update-slice_fusion.12
  155.6 0.7 constant_dynamic-update-slice_fusion.11
  156.3 0.7 constant_dynamic-update-slice_fusion.10
  157.1 0.7 constant_dynamic-update-slice_fusion.9
  157.8 0.7 constant_dynamic-update-slice_fusion.8
  158.5 0.7 constant_dynamic-update-slice_fusion.7
  159.2 0.7 constant_dynamic-update-slice_fusion.6
  160.0 0.7 constant_dynamic-update-slice_fusion.5
  160.7 0.7 constant_dynamic-update-slice_fusion.4
  161.4 0.7 constant_dynamic-update-slice_fusion.3
  162.1 0.8 constant_dynamic-update-slice_fusion.2
  162.9 0.7 constant_dynamic-update-slice_fusion.1
  163.6 0.7 constant_dynamic-update-slice_fusion
  164.3 17.2 %all-gather.6.cloned.1.call-done = bf16[1,1,1024,2048]{3,2,1,0:T(8,128)(2,1)} async-done(((bf16[1,1,64,2048]{3,2,1,0:T(8,128)(2,1)}), bf16[1,1,1024,2048]{3,2,1,0:T(8,128)(2,1)}) %all-gather.6.cloned.1.call-update) | async-done | bytes 4194320 | tf_op jit(solution)/shard_map/all_gather | solution.py:33
  181.6 3.0 %fusion.4 = f32[128,2048]{1,0:T(8,128)S(1)} fusion(bf16[1,1,1024,2048]{3,2,1,0:T(8,128)(2,1)} %all-gather.6.cloned.1.call-done, bf16[64,1024]{1,0:T(8,128)(2,1)} %get-tuple-element.18, bf16[64,1024]{1,0:T(8,128)(2,1)S(1)} %get-tuple-element.17), kind=kOutput, calls=%fused_computation.4 | convolution fusion | flops 537395200 | bytes 5505024 | tf_op jit(solution)/shard_map/dot_general | solution.py:23
  184.6 2.9 %fusion.6 = f32[128,2048]{1,0:T(8,128)S(1)} fusion(bf16[2048,2048]{1,0:T(8,128)(2,1)} %constant_dynamic-update-slice_fusion, s32[]{:T(128)S(6)} %select_n.26, bf16[64,1024]{1,0:T(8,128)(2,1)S(1)} %get-tuple-element.10, bf16[64,1024]{1,0:T(8,128)(2,1)S(1)} %get-tuple-element.9), kind=kOutput, calls=%fused_computation.6 | convolution fusion | flops 537395200 | bytes 5505028 | tf_op jit(solution)/shard_map/dot_general | solution.py:23
  187.6 0.8 fusion.8
  188.6 3.4 %collective-permute-start = (bf16[32,2048]{1,0:T(8,128)(2,1)S(1)}, bf16[32,2048]{1,0:T(8,128)(2,1)S(1)}, u32[]{:S(2)}, u32[]{:S(2)}) collective-permute-start(bf16[32,2048]{1,0:T(8,128)(2,1)S(1)} %add_select_fusion), channel_id=1, source_target_pairs={{0,16},{1,17},{2,18},{3,19},{4,20},{5,21},{6,22},{7,23},{8,24},{9,... | collective-permute-start | bytes 393224 | tf_op jit(solution)/shard_map/ppermute | solution.py:10
  192.0 3.1 %collective-permute-done = bf16[32,2048]{1,0:T(8,128)(2,1)S(1)} collective-permute-done((bf16[32,2048]{1,0:T(8,128)(2,1)S(1)}, bf16[32,2048]{1,0:T(8,128)(2,1)S(1)}, u32[]{:S(2)}, u32[]{:S(2)}) %collective-permute-start) | collective-permute-done | bytes 131104 | tf_op jit(solution)/shard_map/ppermute | solution.py:10
  195.2 42.3 %all-gather.4.cloned.1.call-done = bf16[1024,2048]{1,0:T(8,128)(2,1)} async-done(((bf16[64,2048]{1,0:T(8,128)(2,1)}), bf16[1024,2048]{1,0:T(8,128)(2,1)}) %all-gather.4.cloned.1.call-update) | async-done | bytes 4194320 | tf_op jit(solution)/shard_map/all_gather | solution.py:47
  237.5 3.2 %fusion.22 = f32[64,2048]{1,0:T(8,128)S(1)} fusion(bf16[1024,2048]{1,0:T(8,128)(2,1)} %all-gather.4.cloned.1.call-done, bf16[32,1024]{1,0:T(8,128)(2,1)S(1)} %get-tuple-element.22, bf16[32,1024]{1,0:T(8,128)(2,1)S(1)} %get-tuple-element.21), kind=kOutput, calls=%fused_computation.40 | convolution fusion | flops 268697600 | bytes 4849664 | tf_op jit(solution)/shard_map/dot_general | solution.py:23
  240.9 0.5 slice_bitcast_fusion.1
  241.5 1.4 fusion
  242.9 1.3 collective-permute-start.16
  244.2 6.2 %collective-permute-done.16 = bf16[32,2048]{1,0:T(8,128)(2,1)S(1)} collective-permute-done((bf16[32,2048]{1,0:T(8,128)(2,1)S(1)}, bf16[32,2048]{1,0:T(8,128)(2,1)S(1)}, u32[]{:S(2)}, u32[]{:S(2)}) %collective-permute-start.16) | collective-permute-done | bytes 131104 | tf_op jit(solution)/shard_map/ppermute | solution.py:10
  250.5 0.7 add_bitcast_fusion
  (42 shorter events, 0.7 us)
Async XLA Ops:
  6.5 143.5 %copy-start.1 = (bf16[1,64,2048]{2,1,0:T(8,128)(2,1)S(1)}, bf16[1,64,2048]{2,1,0:T(8,128)(2,1)}, u32[]{:S(2)}) copy-start(bf16[1,64,2048]{2,1,0:T(8,128)(2,1)} %param.5) | copy-start | bytes 786436
  6.5 175.1 %all-gather.6.cloned.1.call-start = ((), (), s32[]{:S(2)}) async-start(), calls=%async_computation.1 | async-start | bytes 4456448 | tf_op jit(solution)/shard_map/all_gather | solution.py:33
  6.5 9.8 %collective-permute-start.1 = (bf16[64,2048]{1,0:T(8,128)(2,1)}, bf16[64,2048]{1,0:T(8,128)(2,1)S(1)}, u32[]{:S(2)}, u32[]{:S(2)}) collective-permute-start(bf16[64,2048]{1,0:T(8,128)(2,1)} %bitcast.16), channel_id=1, source_target_pairs={{0,1},{1,2},{2,3},{3,4},{4,5},{5,6},{6,7},{7,8},{8,9},{9,10},{10,1... | collective-permute-start | bytes 786440 | tf_op jit(solution)/shard_map/ppermute | solution.py:38
  16.3 8.5 %collective-permute-start.2 = (bf16[64,2048]{1,0:T(8,128)(2,1)S(1)}, bf16[64,2048]{1,0:T(8,128)(2,1)S(1)}, u32[]{:S(2)}, u32[]{:S(2)}) collective-permute-start(bf16[64,2048]{1,0:T(8,128)(2,1)S(1)} %collective-permute-done.1), channel_id=1, source_target_pairs={{0,1},{1,2},{2,3},{3,4},{4,5},{5,6},{6,7},{7,8},{8,9},{9,10},{10,1... | collective-permute-start | bytes 786440 | tf_op jit(solution)/shard_map/ppermute | solution.py:38
  24.8 8.5 %collective-permute-start.3 = (bf16[64,2048]{1,0:T(8,128)(2,1)S(1)}, bf16[64,2048]{1,0:T(8,128)(2,1)S(1)}, u32[]{:S(2)}, u32[]{:S(2)}) collective-permute-start(bf16[64,2048]{1,0:T(8,128)(2,1)S(1)} %collective-permute-done.2), channel_id=1, source_target_pairs={{0,1},{1,2},{2,3},{3,4},{4,5},{5,6},{6,7},{7,8},{8,9},{9,10},{10,1... | collective-permute-start | bytes 786440 | tf_op jit(solution)/shard_map/ppermute | solution.py:38
  33.3 8.5 %collective-permute-start.4 = (bf16[64,2048]{1,0:T(8,128)(2,1)S(1)}, bf16[64,2048]{1,0:T(8,128)(2,1)S(1)}, u32[]{:S(2)}, u32[]{:S(2)}) collective-permute-start(bf16[64,2048]{1,0:T(8,128)(2,1)S(1)} %collective-permute-done.3), channel_id=1, source_target_pairs={{0,1},{1,2},{2,3},{3,4},{4,5},{5,6},{6,7},{7,8},{8,9},{9,10},{10,1... | collective-permute-start | bytes 786440 | tf_op jit(solution)/shard_map/ppermute | solution.py:38
  41.8 8.5 %collective-permute-start.5 = (bf16[64,2048]{1,0:T(8,128)(2,1)S(1)}, bf16[64,2048]{1,0:T(8,128)(2,1)S(1)}, u32[]{:S(2)}, u32[]{:S(2)}) collective-permute-start(bf16[64,2048]{1,0:T(8,128)(2,1)S(1)} %collective-permute-done.4), channel_id=1, source_target_pairs={{0,1},{1,2},{2,3},{3,4},{4,5},{5,6},{6,7},{7,8},{8,9},{9,10},{10,1... | collective-permute-start | bytes 786440 | tf_op jit(solution)/shard_map/ppermute | solution.py:38
  50.3 8.5 %collective-permute-start.6 = (bf16[64,2048]{1,0:T(8,128)(2,1)S(1)}, bf16[64,2048]{1,0:T(8,128)(2,1)S(1)}, u32[]{:S(2)}, u32[]{:S(2)}) collective-permute-start(bf16[64,2048]{1,0:T(8,128)(2,1)S(1)} %collective-permute-done.5), channel_id=1, source_target_pairs={{0,1},{1,2},{2,3},{3,4},{4,5},{5,6},{6,7},{7,8},{8,9},{9,10},{10,1... | collective-permute-start | bytes 786440 | tf_op jit(solution)/shard_map/ppermute | solution.py:38
  58.8 8.5 %collective-permute-start.7 = (bf16[64,2048]{1,0:T(8,128)(2,1)S(1)}, bf16[64,2048]{1,0:T(8,128)(2,1)S(1)}, u32[]{:S(2)}, u32[]{:S(2)}) collective-permute-start(bf16[64,2048]{1,0:T(8,128)(2,1)S(1)} %collective-permute-done.6), channel_id=1, source_target_pairs={{0,1},{1,2},{2,3},{3,4},{4,5},{5,6},{6,7},{7,8},{8,9},{9,10},{10,1... | collective-permute-start | bytes 786440 | tf_op jit(solution)/shard_map/ppermute | solution.py:38
  67.3 8.5 %collective-permute-start.8 = (bf16[64,2048]{1,0:T(8,128)(2,1)S(1)}, bf16[64,2048]{1,0:T(8,128)(2,1)S(1)}, u32[]{:S(2)}, u32[]{:S(2)}) collective-permute-start(bf16[64,2048]{1,0:T(8,128)(2,1)S(1)} %collective-permute-done.7), channel_id=1, source_target_pairs={{0,1},{1,2},{2,3},{3,4},{4,5},{5,6},{6,7},{7,8},{8,9},{9,10},{10,1... | collective-permute-start | bytes 786440 | tf_op jit(solution)/shard_map/ppermute | solution.py:38
  75.8 8.5 %collective-permute-start.9 = (bf16[64,2048]{1,0:T(8,128)(2,1)S(1)}, bf16[64,2048]{1,0:T(8,128)(2,1)S(1)}, u32[]{:S(2)}, u32[]{:S(2)}) collective-permute-start(bf16[64,2048]{1,0:T(8,128)(2,1)S(1)} %collective-permute-done.8), channel_id=1, source_target_pairs={{0,1},{1,2},{2,3},{3,4},{4,5},{5,6},{6,7},{7,8},{8,9},{9,10},{10,1... | collective-permute-start | bytes 786440 | tf_op jit(solution)/shard_map/ppermute | solution.py:38
  84.3 8.5 %collective-permute-start.10 = (bf16[64,2048]{1,0:T(8,128)(2,1)S(1)}, bf16[64,2048]{1,0:T(8,128)(2,1)S(1)}, u32[]{:S(2)}, u32[]{:S(2)}) collective-permute-start(bf16[64,2048]{1,0:T(8,128)(2,1)S(1)} %collective-permute-done.9), channel_id=1, source_target_pairs={{0,1},{1,2},{2,3},{3,4},{4,5},{5,6},{6,7},{7,8},{8,9},{9,10},{10,1... | collective-permute-start | bytes 786440 | tf_op jit(solution)/shard_map/ppermute | solution.py:38
  92.8 8.5 %collective-permute-start.11 = (bf16[64,2048]{1,0:T(8,128)(2,1)S(1)}, bf16[64,2048]{1,0:T(8,128)(2,1)S(1)}, u32[]{:S(2)}, u32[]{:S(2)}) collective-permute-start(bf16[64,2048]{1,0:T(8,128)(2,1)S(1)} %collective-permute-done.10), channel_id=1, source_target_pairs={{0,1},{1,2},{2,3},{3,4},{4,5},{5,6},{6,7},{7,8},{8,9},{9,10},{10,1... | collective-permute-start | bytes 786440 | tf_op jit(solution)/shard_map/ppermute | solution.py:38
  101.3 8.5 %collective-permute-start.12 = (bf16[64,2048]{1,0:T(8,128)(2,1)S(1)}, bf16[64,2048]{1,0:T(8,128)(2,1)S(1)}, u32[]{:S(2)}, u32[]{:S(2)}) collective-permute-start(bf16[64,2048]{1,0:T(8,128)(2,1)S(1)} %collective-permute-done.11), channel_id=1, source_target_pairs={{0,1},{1,2},{2,3},{3,4},{4,5},{5,6},{6,7},{7,8},{8,9},{9,10},{10,1... | collective-permute-start | bytes 786440 | tf_op jit(solution)/shard_map/ppermute | solution.py:38
  109.8 8.5 %collective-permute-start.13 = (bf16[64,2048]{1,0:T(8,128)(2,1)S(1)}, bf16[64,2048]{1,0:T(8,128)(2,1)S(1)}, u32[]{:S(2)}, u32[]{:S(2)}) collective-permute-start(bf16[64,2048]{1,0:T(8,128)(2,1)S(1)} %collective-permute-done.12), channel_id=1, source_target_pairs={{0,1},{1,2},{2,3},{3,4},{4,5},{5,6},{6,7},{7,8},{8,9},{9,10},{10,1... | collective-permute-start | bytes 786440 | tf_op jit(solution)/shard_map/ppermute | solution.py:38
  118.3 0.7 copy-start.2
  119.0 8.6 %collective-permute-start.14 = (bf16[64,2048]{1,0:T(8,128)(2,1)S(1)}, bf16[64,2048]{1,0:T(8,128)(2,1)}, u32[]{:S(2)}, u32[]{:S(2)}) collective-permute-start(bf16[64,2048]{1,0:T(8,128)(2,1)S(1)} %collective-permute-done.13), channel_id=1, source_target_pairs={{0,1},{1,2},{2,3},{3,4},{4,5},{5,6},{6,7},{7,8},{8,9},{9,10},{10,1... | collective-permute-start | bytes 786440 | tf_op jit(solution)/shard_map/ppermute | solution.py:38
  127.6 8.8 %collective-permute-start.15 = (bf16[64,2048]{1,0:T(8,128)(2,1)}, bf16[64,2048]{1,0:T(8,128)(2,1)}, u32[]{:S(2)}, u32[]{:S(2)}) collective-permute-start(bf16[64,2048]{1,0:T(8,128)(2,1)} %collective-permute-done.14), channel_id=1, source_target_pairs={{0,1},{1,2},{2,3},{3,4},{4,5},{5,6},{6,7},{7,8},{8,9},{9,10},{10,1... | collective-permute-start | bytes 786440 | tf_op jit(solution)/shard_map/ppermute | solution.py:38
  129.5 108.0 %all-gather.4.cloned.1.call-start = ((), (), s32[]{:S(2)}) async-start(), calls=%async_computation | async-start | bytes 4456448 | tf_op jit(solution)/shard_map/all_gather | solution.py:47
  131.2 23.0 %copy-start.3 = (bf16[64,2048]{1,0:T(8,128)(2,1)S(1)}, bf16[64,2048]{1,0:T(8,128)(2,1)}, u32[]{:S(2)}) copy-start(bf16[64,2048]{1,0:T(8,128)(2,1)} %copy-done.2) | copy-start | bytes 786436
  162.1 26.3 %copy-start.6 = (s32[32]{0:T(128)S(1)}, s32[32]{0:T(128)}, u32[]{:S(2)}) copy-start(s32[32]{0:T(128)} %param.9) | copy-start | bytes 388
  162.1 26.3 %copy-start.5 = (s32[32]{0:T(128)S(1)}, s32[32]{0:T(128)}, u32[]{:S(2)}) copy-start(s32[32]{0:T(128)} %param.8) | copy-start | bytes 388
  162.1 26.5 %copy-start.4 = (bf16[32,2048]{1,0:T(8,128)(2,1)S(1)}, bf16[32,2048]{1,0:T(8,128)(2,1)}, u32[]{:S(2)}) copy-start(bf16[32,2048]{1,0:T(8,128)(2,1)} %param.7) | copy-start | bytes 393220
  188.6 6.5 %collective-permute-start = (bf16[32,2048]{1,0:T(8,128)(2,1)S(1)}, bf16[32,2048]{1,0:T(8,128)(2,1)S(1)}, u32[]{:S(2)}, u32[]{:S(2)}) collective-permute-start(bf16[32,2048]{1,0:T(8,128)(2,1)S(1)} %add_select_fusion), channel_id=1, source_target_pairs={{0,16},{1,17},{2,18},{3,19},{4,20},{5,21},{6,22},{7,23},{8,24},{9,... | collective-permute-start | bytes 393224 | tf_op jit(solution)/shard_map/ppermute | solution.py:10
  237.5 3.4 %copy-start = (bf16[1024,2048]{1,0:T(8,128)(2,1)S(1)}, bf16[1024,2048]{1,0:T(8,128)(2,1)}, u32[]{:S(2)}) copy-start(bf16[1024,2048]{1,0:T(8,128)(2,1)} %all-gather.4.cloned.1.call-done) | copy-start | bytes 12582916
  242.9 7.5 %collective-permute-start.16 = (bf16[32,2048]{1,0:T(8,128)(2,1)S(1)}, bf16[32,2048]{1,0:T(8,128)(2,1)S(1)}, u32[]{:S(2)}, u32[]{:S(2)}) collective-permute-start(bf16[32,2048]{1,0:T(8,128)(2,1)S(1)} %pad_maximum_fusion), channel_id=1, source_target_pairs={{16,0},{17,1},{18,2},{19,3},{20,4},{21,5},{22,6},{23,7},{24,8},{25... | collective-permute-start | bytes 393224 | tf_op jit(solution)/shard_map/ppermute | solution.py:10
Sparse Core Ops, SparseCore 0:
  129.6 51.9 all-gather.5
  188.5 48.9 all-gather.3
